TPU v7x, 128 devices: a whole 4x4x4 slice. The times are simulated.
128 devices in a mesh: pts: 32 (over z, x, core), rep: 4 (over y).
Axes of the slice: x: 4, y: 4, z: 4, core: 2. Of those that a mesh axis runs over, the one named last changes fastest.
Arguments:
- target_xyz: float32 [3, 32768], P(None, 'pts'), may hold values from 0 to 1
- source_xyz: float32 [3, 65536], P(None, ('pts', 'rep')), may hold values from 0 to 1
- target_count: int32 [32], P('pts'), may hold values from 1 to 1024, as said below
- source_count: int32 [128], P(('pts', 'rep')), may hold values from 1 to 512, as said below
- psi: bfloat16 [32768, 256], P('pts'), may hold values from -6 to 6
- omega: bfloat16 [65536, 256], P(('pts', 'rep')), may hold values from -6 to 6
Outputs:
- range_sketch: float32 [32768, 256], P('pts')
- corange_sketch: float32 [65536, 256], P(('pts', 'rep'))
- core: float32 [256, 256], replicated
- range_gram: float32 [256, 256], replicated
- corange_gram: float32 [256, 256], replicated
Inputs may be any that keep to these rules, and one draw needn't show every extreme that they name: `target_count`: each group holds 1 to 1024 live targets; some group holds exactly 1024. `source_count`: each shard holds 1 to 512 live sources; some shard holds exactly 512.
All inputs are finite; a program needn't handle non-finite values.
Results may differ from a plain program's by a relative error of at most 0.0003.
The roundings to bfloat16 on the way count: a program that leaves them out, or rounds other values in their place, can miss the bound.
Values may be sent and summed in bfloat16 or wider, within the bound.
No kernel may reach another device: no remote copies, remote signals or barrier semaphores. Data moves between devices by JAX's collectives and lax.ppermute only.
A program may use at most 64 MiB of HBM per device.

v0:
```python
import math
import jax
import jax.numpy as jnp
from jax import lax
from jax.sharding import PartitionSpec as P

SHIFT = 1.05
SPREAD = 8.0


def tile_block(tgt, src):
    dx = tgt[0][:, None] - (src[0][None, :] + SHIFT)
    dy = SPREAD * (tgt[1][:, None] - src[1][None, :])
    dz = SPREAD * (tgt[2][:, None] - src[2][None, :])
    return lax.rsqrt(dx * dx + dy * dy + dz * dz).astype(jnp.bfloat16)


def local(target_xyz, source_xyz, target_count, source_count, psi, omega):
    tcap = psi.shape[0]
    scap = omega.shape[0]
    width = psi.shape[1]
    n_pts = lax.axis_size("pts")
    n_rep = lax.axis_size("rep")
    all_targets = tcap * n_pts
    all_sources = scap * n_pts * n_rep
    tlive = jnp.arange(tcap, dtype=jnp.int32) < target_count[0]
    slive = jnp.arange(scap, dtype=jnp.int32) < source_count[0]
    psi_live = jnp.where(tlive[:, None], psi, jnp.zeros_like(psi))
    omega_live = jnp.where(slive[:, None], omega, jnp.zeros_like(omega))
    hi = lax.Precision.HIGHEST
    src_all = lax.all_gather(source_xyz, "pts", axis=1, tiled=True)
    piece = lax.all_gather(omega_live, "pts", axis=0, tiled=True)

    def range_inner(j, acc):
        rows = lax.dynamic_slice_in_dim(piece, j * scap, scap, 0)
        where = lax.dynamic_slice_in_dim(src_all, j * scap, scap, 1)
        return acc + jnp.dot(
            tile_block(target_xyz, where), rows, preferred_element_type=jnp.float32
        )

    y_part = lax.fori_loop(
        0, piece.shape[0] // scap, range_inner, jnp.zeros((tcap, width), jnp.float32)
    )
    y_sum = lax.psum(y_part, "rep") * (2.0 / math.sqrt(all_sources))
    range_sketch = jnp.where(tlive[:, None], y_sum, jnp.zeros_like(y_sum))
    tgt_all = lax.all_gather(target_xyz, "pts", axis=1, tiled=True)
    corange_piece = lax.all_gather(psi_live, "pts", axis=0, tiled=True)

    def corange_inner(j, acc):
        rows = lax.dynamic_slice_in_dim(corange_piece, j * tcap, tcap, 0)
        where = lax.dynamic_slice_in_dim(tgt_all, j * tcap, tcap, 1)
        tile = tile_block(where, source_xyz)
        return acc + lax.dot_general(
            tile, rows, (((0,), (0,)), ((), ())), preferred_element_type=jnp.float32
        )

    z_sum = lax.fori_loop(
        0, corange_piece.shape[0] // tcap, corange_inner, jnp.zeros((scap, width), jnp.float32)
    )
    z_scaled = z_sum * (2.0 / math.sqrt(all_targets))
    corange_sketch = jnp.where(slive[:, None], z_scaled, jnp.zeros_like(z_scaled))
    z_gram_part = jnp.dot(corange_sketch.T, corange_sketch, precision=hi)
    core_part = jnp.dot(psi_live.astype(jnp.float32).T, range_sketch, precision=hi)
    y_gram_part = jnp.dot(range_sketch.T, range_sketch, precision=hi)
    core_sum, y_gram = lax.psum((core_part, y_gram_part), "pts")
    z_gram = lax.psum(z_gram_part, ("pts", "rep"))
    core = core_sum / math.sqrt(all_targets)
    range_gram = y_gram / all_targets
    corange_gram = z_gram / all_sources
    return (range_sketch, corange_sketch, core, range_gram, corange_gram)


def solution(mesh):
    return jax.shard_map(
        local,
        mesh=mesh,
        in_specs=(
            P(None, "pts"),
            P(None, ("pts", "rep")),
            P("pts"),
            P(("pts", "rep")),
            P("pts", None),
            P(("pts", "rep"), None),
        ),
        out_specs=(P("pts", None), P(("pts", "rep"), None), P(), P(), P()),
        check_vma=False,
    )
```

profile of v0, /device:TPU:1, one launch (start us, length us, event | category | flops | bytes accessed | tf_op | source)
XLA Modules:
  0.0 550.0 jit_solution(14603858195827019406)
XLA Ops:
  9.7 27.6 %all_gather.12 = f32[3,16384]{1,0:T(4,128)S(1)} all-gather(f32[3,512]{1,0:T(4,128)} %param.11), channel_id=1, replica_groups=mesh['pts'=32,'rep'=4] {'pts'}, dimensions={1}, use_global_device_ids=true | all-gather | bytes 202752 | tf_op jit(solution)/shard_map/all_gather | solution.py:31
  37.3 30.2 %all-gather.3.cloned.1.call-done = bf16[16384,256]{1,0:T(8,128)(2,1)} async-done(((bf16[512,256]{1,0:T(8,128)(2,1)}), bf16[16384,256]{1,0:T(8,128)(2,1)}) %all-gather.3.cloned.1.call-update) | async-done | bytes 8388624 | tf_op jit(solution)/shard_map/all_gather | solution.py:32
  67.5 96.4 %while.28 = (s32[]{:T(128)}, f32[1024,256]{1,0:T(8,128)S(1)}, f32[3,1024]{1,0:T(4,128)}, f32[3,16384]{1,0:T(4,128)S(1)}, bf16[16384,256]{1,0:T(8,128)(2,1)}, /*i...) while((s32[]{:T(128)}, f32[1024,256]{1,0:T(8,128)S(1)}, ...), condition=%wide.region_1.2_spmd.clone, body=%wide.region_0.1_spmd.clone.sunk | while | flops 274727424 | bytes 2414797 | solution.py:41
  68.4 2.0 convolution_add_fusion.4
  83.5 2.0 convolution_add_fusion.4
  86.5 2.0 convolution_add_fusion.4
  119.6 2.0 convolution_add_fusion.4
  122.7 2.0 convolution_add_fusion.4
  134.7 2.0 convolution_add_fusion.4
  166.7 24.7 %all_gather.14 = f32[3,32768]{1,0:T(4,128)S(1)} all-gather(f32[3,1024]{1,0:T(4,128)S(1)} %copy-done.5), channel_id=1, replica_groups=mesh['pts'=32,'rep'=4] {'pts'}, dimensions={1}, use_global_device_ids=true | all-gather | bytes 405504 | tf_op jit(solution)/shard_map/all_gather | solution.py:46
  191.4 17.0 %all-reduce.5.cloned.1.call-done = f32[1024,256]{1,0:T(8,128)} async-done(((f32[1024,256]{1,0:T(8,128)}), f32[1024,256]{1,0:T(8,128)}) %all-reduce.5.cloned.1.call-update) | async-done | bytes 1048592 | tf_op jit(solution)/shard_map/psum | solution.py:44
  211.4 2.6 fusion.22
  214.0 73.1 %all-gather.5.cloned.1.call-done = bf16[32768,256]{1,0:T(8,128)(2,1)} async-done(((bf16[1024,256]{1,0:T(8,128)(2,1)}), bf16[32768,256]{1,0:T(8,128)(2,1)}) %all-gather.5.cloned.1.call-update) | async-done | bytes 16777232 | tf_op jit(solution)/shard_map/all_gather | solution.py:47
  287.1 81.4 %while.29 = (s32[]{:T(128)}, f32[512,256]{1,0:T(8,128)S(1)}, f32[3,32768]{1,0:T(4,128)S(1)}, f32[3,512]{1,0:T(4,128)S(1)}, bf16[32768,256]{1,0:T(8,128)(2,1)}, /...) while((s32[]{:T(128)}, f32[512,256]{1,0:T(8,128)S(1)}, ...), condition=%wide.region_4.5_spmd.clone, body=%wide.region_3.4_spmd.clone.sunk | while | flops 274465280 | bytes 1628365 | solution.py:57
  287.2 2.4 convolution_add_fusion.5
  289.8 2.4 convolution_add_fusion.5
  292.3 2.4 convolution_add_fusion.5
  294.8 2.4 convolution_add_fusion.5
  297.4 2.4 convolution_add_fusion.5
  300.0 2.4 convolution_add_fusion.5
  302.5 2.4 convolution_add_fusion.5
  305.0 2.4 convolution_add_fusion.5
  307.6 2.4 convolution_add_fusion.5
  310.1 2.4 convolution_add_fusion.5
  312.7 2.4 convolution_add_fusion.5
  315.2 2.4 convolution_add_fusion.5
  317.8 2.4 convolution_add_fusion.5
  320.3 2.4 convolution_add_fusion.5
  322.9 2.4 convolution_add_fusion.5
  325.4 2.4 convolution_add_fusion.5
  327.9 2.4 convolution_add_fusion.5
  330.5 2.4 convolution_add_fusion.5
  333.0 2.4 convolution_add_fusion.5
  335.6 2.4 convolution_add_fusion.5
  338.1 2.4 convolution_add_fusion.5
  340.7 2.4 convolution_add_fusion.5
  343.2 2.4 convolution_add_fusion.5
  345.8 2.4 convolution_add_fusion.5
  348.3 2.4 convolution_add_fusion.5
  350.9 2.4 convolution_add_fusion.5
  353.4 2.4 convolution_add_fusion.5
  355.9 2.4 convolution_add_fusion.5
  358.5 2.4 convolution_add_fusion.5
  361.0 2.4 convolution_add_fusion.5
  363.6 2.4 convolution_add_fusion.5
  366.1 2.4 convolution_add_fusion.5
  370.5 24.1 %all-reduce.9.cloned.1.call-done = (f32[256,256]{1,0:T(8,128)}, f32[256,256]{1,0:T(8,128)}) async-done(((f32[256,256]{1,0:T(8,128)}, f32[256,256]{1,0:T(8,128)}), (f32[256,256]{1,0:T(8,128)}, f32[256,256]{1,0:T(8,128)})) %all-reduce.9.cloned.1.call-update) | async-done | bytes 524304 | tf_op jit(solution)/shard_map/psum | solution.py:65
  396.4 145.4 %all-reduce.7.cloned.1.call-done = f32[256,256]{1,0:T(8,128)} async-done(((f32[256,256]{1,0:T(8,128)}), f32[256,256]{1,0:T(8,128)}) %all-reduce.7.cloned.1.call-update) | async-done | bytes 262160 | tf_op jit(solution)/shard_map/psum | solution.py:66
  (190 shorter events, 98.5 us)
Async XLA Ops:
  7.2 60.3 %all-gather.3.cloned.1.call-start = ((), (), s32[]{:S(2)}) async-start(), calls=%async_computation | async-start | bytes 8650752 | tf_op jit(solution)/shard_map/all_gather | solution.py:32
  9.7 198.7 %all-reduce.5.cloned.1.call-start = ((), (), s32[]{:S(2)}) async-start(), calls=%async_computation.1 | async-start | bytes 2097152 | tf_op jit(solution)/shard_map/psum | solution.py:44
  67.5 98.1 %copy-start.4 = (bf16[1024,256]{1,0:T(8,128)(2,1)S(1)}, bf16[1024,256]{1,0:T(8,128)(2,1)}, u32[]{:S(2)}) copy-start(bf16[1024,256]{1,0:T(8,128)(2,1)} %param.14) | copy-start | bytes 1572868
  163.9 1.0 copy-start.3
  163.9 2.8 copy-start.5
  164.9 122.2 %all-gather.5.cloned.1.call-start = ((), (), s32[]{:S(2)}) async-start(), calls=%async_computation.2 | async-start | bytes 17301504 | tf_op jit(solution)/shard_map/all_gather | solution.py:47
  166.6 43.2 %copy-start.2 = (bf16[1024,256]{1,0:T(8,128)(2,1)S(1)}, bf16[1024,256]{1,0:T(8,128)(2,1)}, u32[]{:S(2)}) copy-start(bf16[1024,256]{1,0:T(8,128)(2,1)} %broadcast_select_fusion) | copy-start | bytes 1572868
  166.6 227.9 %all-reduce.9.cloned.1.call-start = ((), (), s32[]{:S(2)}) async-start(), calls=%async_computation.4 | async-start | bytes 1048576 | tf_op jit(solution)/shard_map/psum | solution.py:65
  209.8 4.1 copy-start
  209.9 77.3 %copy-start.6 = (f32[3,512]{1,0:T(4,128)S(1)}, f32[3,512]{1,0:T(4,128)}, u32[]{:S(2)}) copy-start(f32[3,512]{1,0:T(4,128)} %param.11) | copy-start | bytes 18436
  214.0 327.8 %all-reduce.7.cloned.1.call-start = ((), (), s32[]{:S(2)}) async-start(), calls=%async_computation.3 | async-start | bytes 524288 | tf_op jit(solution)/shard_map/psum | solution.py:66
  368.7 174.8 %copy-start.1 = (f32[512,256]{1,0:T(8,128)}, f32[512,256]{1,0:T(8,128)S(1)}, u32[]{:S(2)}) copy-start(f32[512,256]{1,0:T(8,128)S(1)} %multiply_select_fusion.1) | copy-start | bytes 1572868
Sparse Core Ops, SparseCore 0:
  10.8 56.6 all-gather.2
  165.0 43.3 all-reduce.4
  211.2 75.8 all-gather.4
  290.8 103.6 all-reduce.8
  399.1 142.5 all-reduce.6
where the time goes:
time: 555 us; the launch traced here: 550 us
  waiting for transfers between devices  290 us (52%)
  matrix products  148 us (27%)
  blocking collectives  52.2 us (9%)
  local copies, waits for them, and re-layouts  30.9 us (6%)
  between operations  15.2 us (3%)
  other arithmetic  10.8 us (2%)
    psum x1, waiting for transfers between devices, local(): z_gram = lax.psum(z_gram_part, ('pts', 'rep'))  145 us
    dot_general x32, matrix products, corange_inner(): lax.dot_general(tile, rows, (((0,), (0,)), ((), ())), preferred_element_t...  76.9 us
    all_gather x1, waiting for transfers between devices, local(): corange_piece = lax.all_gather(psi_live, 'pts', axis=0, tiled=True)  73.1 us
    dot_general x32, matrix products, range_inner(): jnp.dot(tile_block(target_xyz, where), rows, preferred_element_type=jnp.f...  65.5 us
    all_gather x1, waiting for transfers between devices, local(): piece = lax.all_gather(omega_live, 'pts', axis=0, tiled=True)  30.2 us
    slice x64, local copies, waits for them, and re-layouts, tile_block(): dx = tgt[0][:, None] - (src[0][None, :] + SHIFT)  30 us
    all_gather x1, blocking collectives, local(): src_all = lax.all_gather(source_xyz, 'pts', axis=1, tiled=True)  27.6 us
    all_gather x1, blocking collectives, local(): tgt_all = lax.all_gather(target_xyz, 'pts', axis=1, tiled=True)  24.7 us
  transfers between devices with their start and end apart: 5, of which 5 were waited for; matrix products, arithmetic and copies ran while one was open for 16% of the time, Pallas kernels for 0%

commit v1 on v0

--- a/solution.py
+++ b/solution.py
@@ -6,6 +6,12 @@
 
 SHIFT = 1.05
 SPREAD = 8.0
+
+
+def gather_and_add(value, axis):
+    parts = lax.all_gather(value, axis, axis=0, tiled=False)
+    result = parts.sum(axis=0)
+    return result
 
 
 def tile_block(tgt, src):
@@ -63,7 +69,7 @@
     core_part = jnp.dot(psi_live.astype(jnp.float32).T, range_sketch, precision=hi)
     y_gram_part = jnp.dot(range_sketch.T, range_sketch, precision=hi)
     core_sum, y_gram = lax.psum((core_part, y_gram_part), "pts")
-    z_gram = lax.psum(z_gram_part, ("pts", "rep"))
+    z_gram = gather_and_add(z_gram_part, ("pts", "rep"))
     core = core_sum / math.sqrt(all_targets)
     range_gram = y_gram / all_targets
     corange_gram = z_gram / all_sources

time: 555 us -> 528 us (0.951)
  waiting for transfers between devices: 290 us -> 252 us
  other arithmetic: 10.8 us -> 21.9 us
    psum x1 -> x0, waiting for transfers between devices: 145 us -> none  [local(): z_gram = lax.psum(z_gram_part, ('pts', 'rep'))]
    all_gather x0 -> x1, waiting for transfers between devices: none -> 107 us  [gather_and_add(): parts = lax.all_gather(value, axis, axis=0, tiled=False)]
    reduce_sum x0 -> x1, other arithmetic: none -> 12 us  [gather_and_add(): result = parts.sum(axis=0)]
  transfers between devices with their start and end apart: 5 -> 5, of which waited for: 5 -> 5; matrix products, arithmetic and copies ran while one was open for 16% -> 17% of each run, Pallas kernels for 0% -> 0%
where the time goes in v1:
time: 528 us; the launch traced here: 523 us
  waiting for transfers between devices  252 us (48%)
  matrix products  148 us (28%)
  blocking collectives  52.2 us (10%)
  local copies, waits for them, and re-layouts  30.9 us (6%)
  other arithmetic  21.9 us (4%)
  between operations  15.2 us (3%)
    all_gather x1, waiting for transfers between devices, gather_and_add(): parts = lax.all_gather(value, axis, axis=0, tiled=False)  107 us
    dot_general x32, matrix products, corange_inner(): lax.dot_general(tile, rows, (((0,), (0,)), ((), ())), preferred_element_t...  76.9 us
    all_gather x1, waiting for transfers between devices, local(): corange_piece = lax.all_gather(psi_live, 'pts', axis=0, tiled=True)  73.1 us
    dot_general x32, matrix products, range_inner(): jnp.dot(tile_block(target_xyz, where), rows, preferred_element_type=jnp.f...  65.5 us
    all_gather x1, waiting for transfers between devices, local(): piece = lax.all_gather(omega_live, 'pts', axis=0, tiled=True)  30.2 us
    slice x64, local copies, waits for them, and re-layouts, tile_block(): dx = tgt[0][:, None] - (src[0][None, :] + SHIFT)  30 us
    all_gather x1, blocking collectives, local(): src_all = lax.all_gather(source_xyz, 'pts', axis=1, tiled=True)  27.6 us
    all_gather x1, blocking collectives, local(): tgt_all = lax.all_gather(target_xyz, 'pts', axis=1, tiled=True)  24.7 us
  transfers between devices with their start and end apart: 5, of which 5 were waited for; matrix products, arithmetic and copies ran while one was open for 17% of the time, Pallas kernels for 0%

profile of v1, /device:TPU:1, one launch (start us, length us, event | category | flops | bytes accessed | tf_op | source)
XLA Modules:
  0.0 523.1 jit_solution(4474977850387014837)
XLA Ops:
  9.7 27.6 %all_gather.18 = f32[3,16384]{1,0:T(4,128)S(1)} all-gather(f32[3,512]{1,0:T(4,128)} %param.11), channel_id=1, replica_groups=mesh['pts'=32,'rep'=4] {'pts'}, dimensions={1}, use_global_device_ids=true | all-gather | bytes 202752 | tf_op jit(solution)/shard_map/all_gather | solution.py:37
  37.3 30.2 %all-gather.5.cloned.1.call-done = bf16[16384,256]{1,0:T(8,128)(2,1)} async-done(((bf16[512,256]{1,0:T(8,128)(2,1)}), bf16[16384,256]{1,0:T(8,128)(2,1)}) %all-gather.5.cloned.1.call-update) | async-done | bytes 8388624 | tf_op jit(solution)/shard_map/all_gather | solution.py:38
  67.5 96.4 %while.28 = (s32[]{:T(128)}, f32[1024,256]{1,0:T(8,128)S(1)}, f32[3,1024]{1,0:T(4,128)}, f32[3,16384]{1,0:T(4,128)S(1)}, bf16[16384,256]{1,0:T(8,128)(2,1)}, /*i...) while((s32[]{:T(128)}, f32[1024,256]{1,0:T(8,128)S(1)}, ...), condition=%wide.region_1.2_spmd.clone, body=%wide.region_0.1_spmd.clone.sunk | while | flops 274727424 | bytes 2414797 | solution.py:47
  68.4 2.0 convolution_add_fusion.4
  83.5 2.0 convolution_add_fusion.4
  86.5 2.0 convolution_add_fusion.4
  119.6 2.0 convolution_add_fusion.4
  122.7 2.0 convolution_add_fusion.4
  166.7 24.7 %all_gather.20 = f32[3,32768]{1,0:T(4,128)S(1)} all-gather(f32[3,1024]{1,0:T(4,128)S(1)} %copy-done.5), channel_id=1, replica_groups=mesh['pts'=32,'rep'=4] {'pts'}, dimensions={1}, use_global_device_ids=true | all-gather | bytes 405504 | tf_op jit(solution)/shard_map/all_gather | solution.py:52
  191.4 17.0 %all-reduce.4.cloned.1.call-done = f32[1024,256]{1,0:T(8,128)} async-done(((f32[1024,256]{1,0:T(8,128)}), f32[1024,256]{1,0:T(8,128)}) %all-reduce.4.cloned.1.call-update) | async-done | bytes 1048592 | tf_op jit(solution)/shard_map/psum | solution.py:50
  211.4 2.6 fusion.22
  214.0 73.1 %all-gather.7.cloned.1.call-done = bf16[32768,256]{1,0:T(8,128)(2,1)} async-done(((bf16[1024,256]{1,0:T(8,128)(2,1)}), bf16[32768,256]{1,0:T(8,128)(2,1)}) %all-gather.7.cloned.1.call-update) | async-done | bytes 16777232 | tf_op jit(solution)/shard_map/all_gather | solution.py:53
  287.1 81.4 %while.29 = (s32[]{:T(128)}, f32[512,256]{1,0:T(8,128)S(1)}, f32[3,32768]{1,0:T(4,128)S(1)}, f32[3,512]{1,0:T(4,128)S(1)}, bf16[32768,256]{1,0:T(8,128)(2,1)}, /...) while((s32[]{:T(128)}, f32[512,256]{1,0:T(8,128)S(1)}, ...), condition=%wide.region_4.5_spmd.clone, body=%wide.region_3.4_spmd.clone.sunk | while | flops 274465280 | bytes 1628365 | solution.py:63
  287.2 2.4 convolution_add_fusion.5
  289.8 2.4 convolution_add_fusion.5
  292.3 2.4 convolution_add_fusion.5
  294.8 2.4 convolution_add_fusion.5
  297.4 2.4 convolution_add_fusion.5
  300.0 2.4 convolution_add_fusion.5
  302.5 2.4 convolution_add_fusion.5
  305.0 2.4 convolution_add_fusion.5
  307.6 2.4 convolution_add_fusion.5
  310.1 2.4 convolution_add_fusion.5
  312.7 2.4 convolution_add_fusion.5
  315.2 2.4 convolution_add_fusion.5
  317.8 2.4 convolution_add_fusion.5
  320.3 2.4 convolution_add_fusion.5
  322.9 2.4 convolution_add_fusion.5
  325.4 2.4 convolution_add_fusion.5
  327.9 2.4 convolution_add_fusion.5
  330.5 2.4 convolution_add_fusion.5
  333.0 2.4 convolution_add_fusion.5
  335.6 2.4 convolution_add_fusion.5
  338.1 2.4 convolution_add_fusion.5
  340.7 2.4 convolution_add_fusion.5
  343.2 2.4 convolution_add_fusion.5
  345.8 2.4 convolution_add_fusion.5
  348.3 2.4 convolution_add_fusion.5
  350.9 2.4 convolution_add_fusion.5
  353.4 2.4 convolution_add_fusion.5
  355.9 2.4 convolution_add_fusion.5
  358.5 2.4 convolution_add_fusion.5
  361.0 2.4 convolution_add_fusion.5
  363.6 2.4 convolution_add_fusion.5
  366.1 2.4 convolution_add_fusion.5
  370.5 24.1 %all-reduce.6.cloned.1.call-done = (f32[256,256]{1,0:T(8,128)}, f32[256,256]{1,0:T(8,128)}) async-done(((f32[256,256]{1,0:T(8,128)}, f32[256,256]{1,0:T(8,128)}), (f32[256,256]{1,0:T(8,128)}, f32[256,256]{1,0:T(8,128)})) %all-reduce.6.cloned.1.call-update) | async-done | bytes 524304 | tf_op jit(solution)/shard_map/psum | solution.py:71
  396.4 107.4 %all-gather.9.cloned.1.call-done = f32[32768,256]{1,0:T(8,128)} async-done(((f32[256,256]{1,0:T(8,128)}), f32[32768,256]{1,0:T(8,128)}) %all-gather.9.cloned.1.call-update) | async-done | bytes 33554448 | tf_op jit(solution)/shard_map/all_gather | solution.py:12
  503.8 12.0 %reduce_sum.9 = f32[256,256]{1,0:T(8,128)S(1)} reduce(f32[128,256,256]{2,1,0:T(8,128)} %bitcast.47, f32[]{:T(128)} %constant.95.clone.1), dimensions={0}, to_apply=%region_7.8 | reduce | flops 8323072 | bytes 33816580 | tf_op jit(solution)/shard_map/reduce_sum | solution.py:13
  (191 shorter events, 99.6 us)
Async XLA Ops:
  7.2 60.3 %all-gather.5.cloned.1.call-start = ((), (), s32[]{:S(2)}) async-start(), calls=%async_computation | async-start | bytes 8650752 | tf_op jit(solution)/shard_map/all_gather | solution.py:38
  9.7 198.7 %all-reduce.4.cloned.1.call-start = ((), (), s32[]{:S(2)}) async-start(), calls=%async_computation.1 | async-start | bytes 2097152 | tf_op jit(solution)/shard_map/psum | solution.py:50
  67.5 98.1 %copy-start.4 = (bf16[1024,256]{1,0:T(8,128)(2,1)S(1)}, bf16[1024,256]{1,0:T(8,128)(2,1)}, u32[]{:S(2)}) copy-start(bf16[1024,256]{1,0:T(8,128)(2,1)} %param.14) | copy-start | bytes 1572868
  163.9 1.0 copy-start.3
  163.9 2.8 copy-start.5
  164.9 122.2 %all-gather.7.cloned.1.call-start = ((), (), s32[]{:S(2)}) async-start(), calls=%async_computation.2 | async-start | bytes 17301504 | tf_op jit(solution)/shard_map/all_gather | solution.py:53
  166.6 43.2 %copy-start.2 = (bf16[1024,256]{1,0:T(8,128)(2,1)S(1)}, bf16[1024,256]{1,0:T(8,128)(2,1)}, u32[]{:S(2)}) copy-start(bf16[1024,256]{1,0:T(8,128)(2,1)} %broadcast_select_fusion) | copy-start | bytes 1572868
  166.6 227.9 %all-reduce.6.cloned.1.call-start = ((), (), s32[]{:S(2)}) async-start(), calls=%async_computation.4 | async-start | bytes 1048576 | tf_op jit(solution)/shard_map/psum | solution.py:71
  209.8 4.1 copy-start
  209.9 77.3 %copy-start.6 = (f32[3,512]{1,0:T(4,128)S(1)}, f32[3,512]{1,0:T(4,128)}, u32[]{:S(2)}) copy-start(f32[3,512]{1,0:T(4,128)} %param.11) | copy-start | bytes 18436
  214.0 289.8 %all-gather.9.cloned.1.call-start = ((), (), s32[]{:S(2)}) async-start(), calls=%async_computation.3 | async-start | bytes 33816576 | tf_op jit(solution)/shard_map/all_gather | solution.py:12
  368.7 147.1 %copy-start.1 = (f32[512,256]{1,0:T(8,128)}, f32[512,256]{1,0:T(8,128)S(1)}, u32[]{:S(2)}) copy-start(f32[512,256]{1,0:T(8,128)S(1)} %multiply_select_fusion.1) | copy-start | bytes 1572868
Sparse Core Ops, SparseCore 0:
  10.8 56.6 all-gather.4
  165.0 43.3 all-reduce.3
  211.2 75.8 all-gather.6
  290.8 103.6 all-reduce.5
  397.5 106.2 all-gather.8
